TPU v7x, 128 devices: a whole 4x4x4 slice. The times are simulated.
128 devices in a mesh: section: 2 (over z_lo), dp: 8 (over z_hi, y), ctx: 8 (over x, core).
Axes of the slice: x: 4, y: 4, z: 4 (z_hi: 2, z_lo: 2; z = z_hi * 2 + z_lo), core: 2. Of those that a mesh axis runs over, the one named last changes fastest.
Arguments:
- token_ids: int32 [2048], P('ctx'), may hold values from 0 to 511
- embedding: bfloat16 [512, 4096], P(None, 'dp'), may hold values from -6 to 6
- project_in: bfloat16 [2, 4096, 3, 4096], P('section', 'ctx', None, 'dp'), may hold values from -0.09375 to 0.09375
- short_taps: float32 [2, 3, 3, 4096], P('section', None, None, 'dp'), may hold values from -3.5 to 3.5
- filter_taps: float32 [2, 128, 4096], P('section', None, 'dp'), may hold values from -0.5 to 0.5
- decay_rates: float32 [2, 4096], P('section', 'dp'), may hold values from 0.5 to 4
- project_out: bfloat16 [2, 4096, 4096], P('section', 'dp', 'ctx'), may hold values from -0.09375 to 0.09375
- cotangent: bfloat16 [2048, 4096], P('ctx', 'dp'), may hold values from -0.125 to 0.125
Outputs:
- grad_project_in: float32 [2, 4096, 3, 4096], P('section', 'ctx', None, 'dp')
- grad_project_out: float32 [2, 4096, 4096], P('section', 'dp', 'ctx')
- grad_filter: float32 [2, 128, 4096], P('section', None, 'dp')
- grad_decay: float32 [2, 4096], P('section', 'dp')
- grad_short: float32 [2, 3, 3, 4096], P('section', None, None, 'dp')
All inputs are finite; a program needn't handle non-finite values.
Results may differ from a plain program's by a relative error of at most 0.03.
Values may be sent and summed in bfloat16 or wider, within the bound.
A program may use at most 128 MiB of HBM per device.

v0:
```python
import jax
import jax.numpy as jnp
from jax import lax
from jax.sharding import PartitionSpec as P

EPSILON = 1e-06


def gather_turned(arrays, axis, dims):
    turned = [jnp.moveaxis(a, dim, 0) for a, dim in zip(arrays, dims)]
    both = jnp.concatenate([t.reshape(len(t), -1) for t in turned], axis=1)
    filled, at, finished = (lax.all_gather(both, axis, axis=0, tiled=True), 0, [])
    for t, dim in zip(turned, dims):
        section = filled[:, at : at + t[0].size].reshape(-1, *t.shape[1:])
        finished.append(jnp.moveaxis(section, 0, dim))
        at += t[0].size
    return tuple(finished)


def laid_out(pieces, dim):
    pieces = jnp.moveaxis(pieces, 0, dim)
    shape = pieces.shape
    return pieces.reshape(*shape[:dim], shape[dim] * shape[dim + 1], *shape[dim + 2 :])


def from_everyone(shard, axis):
    copies = jnp.broadcast_to(shard, (lax.axis_size(axis), *shard.shape))
    return lax.all_to_all(copies, axis, split_axis=0, concat_axis=0, tiled=True)


def gather_directly(shard, axis, dim):
    return laid_out(from_everyone(shard, axis), dim)


def from_behind(value, axis, steps):
    count = lax.axis_size(axis)
    initial, last = (max(0, -steps), min(count, count - steps))
    return lax.ppermute(value, axis, [(source, source + steps) for source in range(initial, last)])


def cut_along(shard, dim, peers):
    shape = shard.shape
    pieces = shard.reshape(*shape[:dim], peers, shape[dim] // peers, *shape[dim + 1 :])
    return jnp.moveaxis(pieces, dim, 0)


def summed_on_arrival(shard, axis, dim):
    peers = lax.axis_size(axis)
    pieces = lax.all_to_all(cut_along(shard, dim, peers), axis, 0, 0, tiled=True)
    return jnp.sum(pieces.astype(jnp.float32), axis=0)


def taken_together(shard, axis):
    everything = from_everyone(shard, axis)
    return jnp.sum(everything, axis=0)


def over_copies(shard, axis):
    everything = from_everyone(shard, axis)
    return jnp.sum(everything.astype(jnp.float32), axis=0)


def correlate(signal, kernel):
    channels = signal.shape[1]
    result = lax.conv_general_dilated(
        signal[None],
        kernel[:, None, :],
        (1,),
        "VALID",
        dimension_numbers=("NWC", "WIO", "NWC"),
        feature_group_count=channels,
        precision=lax.Precision.HIGHEST,
    )
    return result[0]


def local(
    token_ids, embedding, project_in, short_taps, filter_taps, decay_rates, project_out, cotangent
):
    section_zero = lax.axis_index("section") == 0
    tok_rows = token_ids.shape[0]
    weights_in, weights_out = gather_turned((project_in[0], project_out[0]), "ctx", (0, 1))
    full_width = weights_in.shape[0]
    chan_count = weights_in.shape[2]
    flat_in = weights_in.reshape(full_width, 3 * chan_count)
    taps_local = short_taps[0]
    filter_local = filter_taps[0]
    tap_count = filter_local.shape[0]
    positions = jnp.arange(tap_count).astype(jnp.float32)
    damping = jnp.exp(-decay_rates[0][None, :] * positions[:, None] / tap_count)
    kernel = filter_local * damping
    onehot = (
        token_ids[:, None] == jnp.arange(embedding.shape[0], dtype=jnp.int32)[None, :]
    ).astype(jnp.bfloat16)
    first_input = jnp.dot(onehot, embedding, preferred_element_type=jnp.float32).astype(
        jnp.bfloat16
    )

    def forward(inputs, apply_out):
        rows_all = gather_directly(inputs, "dp", 1)
        rows_float = rows_all.astype(jnp.float32)
        inv_rms = lax.rsqrt(jnp.mean(rows_float * rows_float, axis=1, keepdims=True) + EPSILON)
        normed = (rows_float * inv_rms).astype(jnp.bfloat16)
        projected = jnp.dot(normed, flat_in, preferred_element_type=jnp.float32).reshape(
            tok_rows, 3, chan_count
        )
        earlier = from_behind(projected[tok_rows - 2 :], "ctx", 1)
        padded_proj = jnp.concatenate([earlier, projected], axis=0)
        shortened = (
            taps_local[0] * padded_proj[2:]
            + taps_local[1] * padded_proj[1:-1]
            + taps_local[2] * padded_proj[:-2]
        )
        products = shortened[:, 1] * shortened[:, 2]
        earlier_prod = from_behind(
            products[tok_rows - tap_count + 1 :].astype(jnp.bfloat16), "ctx", 1
        ).astype(jnp.float32)
        padded_prod = jnp.concatenate([earlier_prod, products], axis=0)
        filtered = correlate(padded_prod, kernel[::-1])
        gated_rows = (shortened[:, 0] * filtered).astype(jnp.bfloat16)
        saved = (
            inputs,
            rows_float,
            inv_rms,
            normed,
            padded_proj,
            shortened,
            padded_prod,
            filtered,
            gated_rows,
        )
        if apply_out:
            partials = jnp.dot(gated_rows, weights_out, preferred_element_type=jnp.float32)
            summed = summed_on_arrival(partials.astype(jnp.bfloat16), "dp", 1)
            return ((inputs.astype(jnp.float32) + summed).astype(jnp.bfloat16), saved)
        return (None, saved)

    def backward(saved, grad_local, need_input):
        (
            inputs,
            rows_float,
            inv_rms,
            normed,
            padded_proj,
            shortened,
            padded_prod,
            filtered,
            gated_rows,
        ) = saved
        grad_rows = gather_directly(grad_local, "dp", 1)
        grad_gated = lax.dot_general(
            grad_rows, weights_out, (((1,), (1,)), ((), ())), preferred_element_type=jnp.float32
        )
        grad_query = grad_gated * filtered
        grad_filtered = grad_gated * shortened[:, 0]
        later_rows = from_behind(
            grad_filtered[: tap_count - 1].astype(jnp.bfloat16), "ctx", -1
        ).astype(jnp.float32)
        grad_prod = correlate(jnp.concatenate([grad_filtered, later_rows], axis=0), kernel)
        grad_kernel = correlate(padded_prod, grad_filtered)[::-1]
        grad_short_out = jnp.stack(
            [grad_query, grad_prod * shortened[:, 2], grad_prod * shortened[:, 1]], axis=1
        )
        later_short = from_behind(grad_short_out[:2], "ctx", -1)
        padded_short = jnp.concatenate([grad_short_out, later_short], axis=0)
        grad_proj = (
            taps_local[0] * padded_short[:-2]
            + taps_local[1] * padded_short[1:-1]
            + taps_local[2] * padded_short[2:]
        )
        grad_taps = jnp.stack(
            [
                jnp.sum(grad_short_out * padded_proj[2:], axis=0),
                jnp.sum(grad_short_out * padded_proj[1:-1], axis=0),
                jnp.sum(grad_short_out * padded_proj[:-2], axis=0),
            ],
            axis=0,
        )
        grad_proj_b = grad_proj.astype(jnp.bfloat16)
        grad_inputs = None
        if need_input:
            partials = lax.dot_general(
                grad_proj_b.reshape(tok_rows, 3 * chan_count),
                flat_in,
                (((1,), (1,)), ((), ())),
                preferred_element_type=jnp.float32,
            )
            shared_part = summed_on_arrival(partials.astype(jnp.bfloat16), "dp", 1)
            own_rows = inputs.astype(jnp.float32)
            row_stat = (
                taken_together(jnp.sum(own_rows * shared_part, axis=1), "dp")[:, None] / full_width
            )
            local_grad = inv_rms * shared_part - own_rows * inv_rms**3 * row_stat
            grad_inputs = (grad_local.astype(jnp.float32) + local_grad).astype(jnp.bfloat16)
        return (grad_inputs, (normed, gated_rows, grad_rows, grad_proj_b, grad_kernel, grad_taps))

    out_first, saved_first = forward(first_input, True)
    arrived = from_behind(out_first, "section", 1)
    unused_out, saved_second = forward(arrived, False)
    back_grad, late_parts = backward(saved_second, cotangent, True)
    returned = from_behind(back_grad, "section", -1)
    unused_grad, early_parts = backward(saved_first, returned, False)
    normed, gated_rows, grad_rows, grad_proj_b, grad_kernel, grad_taps = tuple(
        (
            jnp.where(section_zero, early_item, late_item)
            for early_item, late_item in zip(early_parts, late_parts)
        )
    )
    kernel_sum, taps_sum = (
        over_copies(grad_kernel.astype(jnp.bfloat16), "ctx").astype(jnp.float32),
        over_copies(grad_taps.astype(jnp.bfloat16), "ctx").astype(jnp.float32),
    )
    grad_filter = kernel_sum * damping
    grad_decay = (
        -jnp.sum(kernel_sum * filter_local * damping * positions[:, None], axis=0) / tap_count
    )
    flat_grad = grad_proj_b.reshape(tok_rows, 3 * chan_count)
    row_block = lax.slice_in_dim(
        normed, 0, full_width // lax.axis_size("ctx") * lax.axis_size("ctx"), axis=1
    )
    grad_in = lax.psum_scatter(
        lax.dot_general(
            row_block, flat_grad, (((0,), (0,)), ((), ())), preferred_element_type=jnp.float32
        )
        .reshape(full_width // lax.axis_size("ctx") * lax.axis_size("ctx"), 3, chan_count)
        .astype(jnp.bfloat16),
        "ctx",
        scatter_dimension=0,
        tiled=True,
    ).astype(jnp.float32)
    out_partials = lax.dot_general(
        gated_rows, grad_rows, (((0,), (0,)), ((), ())), preferred_element_type=jnp.float32
    )
    grad_out = summed_on_arrival(out_partials.astype(jnp.bfloat16), "ctx", 1)
    return (grad_in[None], grad_out[None], grad_filter[None], grad_decay[None], taps_sum[None])


def solution(mesh):
    return jax.shard_map(
        local,
        mesh=mesh,
        in_specs=(
            P("ctx"),
            P(None, "dp"),
            P("section", "ctx", None, "dp"),
            P("section", None, None, "dp"),
            P("section", None, "dp"),
            P("section", "dp"),
            P("section", "dp", "ctx"),
            P("ctx", "dp"),
        ),
        out_specs=(
            P("section", "ctx", None, "dp"),
            P("section", "dp", "ctx"),
            P("section", None, "dp"),
            P("section", "dp"),
            P("section", None, None, "dp"),
        ),
        check_vma=False,
    )
```

profile of v0, /device:TPU:1, one launch (start us, length us, event | category | flops | bytes accessed | tf_op | source)
XLA Modules:
  0.0 550.6 jit_solution(13177721387538396610)
XLA Ops:
  13.2 8.5 %all-to-all-start = ((bf16[8,256,512]{1,2,0:T(8,128)(2,1)}), bf16[8,256,512]{1,2,0:T(8,128)(2,1)S(1)}, u32[]{:S(2)}, u32[]{:S(2)}) async-start(bf16[8,256,512]{1,2,0:T(8,128)(2,1)} %broadcast_in_dim.68), calls=%async_computation | async-start | bytes 4194304 | tf_op jit(solution)/shard_map/all_to_all | solution.py:28
  21.9 28.4 %all-to-all-done = bf16[8,256,512]{1,2,0:T(8,128)(2,1)S(1)} async-done(((bf16[8,256,512]{1,2,0:T(8,128)(2,1)}), bf16[8,256,512]{1,2,0:T(8,128)(2,1)S(1)}, u32[]{:S(2)}, u32[]{:S(2)}) %all-to-all-start) | async-done | bytes 2097184 | tf_op jit(solution)/shard_map/all_to_all | solution.py:28
  52.7 46.5 %all-gather.2.cloned.1.call-done = bf16[4096,2048]{0,1:T(8,128)(2,1)} async-done(((bf16[512,2048]{0,1:T(8,128)(2,1)}), bf16[4096,2048]{0,1:T(8,128)(2,1)}) %all-gather.2.cloned.1.call-update) | async-done | bytes 16777232 | tf_op jit(solution)/shard_map/all_gather | solution.py:12
  99.2 7.1 %fusion.4 = f32[256,1536]{1,0:T(8,128)S(1)} fusion(bf16[256,4096]{0,1:T(8,128)(2,1)} %fusion.10, bf16[4096,2048]{0,1:T(8,128)(2,1)} %all-gather.2.cloned.1.call-done), kind=kOutput, calls=%fused_computation.4 | convolution fusion | flops 3221225472 | bytes 16252928 | tf_op jit(solution)/shard_map/dot_general | solution.py:104
  125.7 5.3 fusion.64
  134.9 35.3 %all_to_all.51 = bf16[8,256,512]{2,1,0:T(8,128)(2,1)S(1)} all-to-all(bf16[8,256,512]{2,1,0:T(8,128)(2,1)S(1)} %bitcast.181), channel_id=1, replica_groups=mesh['section'=2,'dp'=8,'ctx'=8] {'dp'}, dimensions={0} | all-to-all | bytes 4194304 | tf_op jit(solution)/shard_map/all_to_all | solution.py:49
  172.9 5.2 collective-permute-done.2
  179.7 4.5 all-to-all-start.2
  184.4 28.5 %all-to-all-done.2 = bf16[8,256,512]{1,2,0:T(8,128)(2,1)} async-done(((bf16[8,256,512]{1,2,0:T(8,128)(2,1)}), bf16[8,256,512]{1,2,0:T(8,128)(2,1)}, u32[]{:S(2)}, u32[]{:S(2)}) %all-to-all-start.2) | async-done | bytes 2097184 | tf_op jit(solution)/shard_map/all_to_all | solution.py:28
  214.3 4.3 all-to-all-start.3
  223.4 6.5 %fusion.2 = f32[256,1536]{1,0:T(8,128)S(1)} fusion(bf16[256,4096]{0,1:T(8,128)(2,1)S(1)} %fusion.9, bf16[4096,2048]{0,1:T(8,128)(2,1)} %all-gather.2.cloned.1.call-done), kind=kOutput, calls=%fused_computation.2 | convolution fusion | flops 3221225472 | bytes 16252928 | tf_op jit(solution)/shard_map/dot_general | solution.py:104
  239.1 4.3 multiply_add_fusion
  243.4 3.9 all-to-all-done.3
  247.3 4.2 bitcast_multiply_fusion.11
  257.9 5.3 fusion.32
  267.4 5.3 fusion.49
  282.0 8.3 %fusion.6 = bf16[256,4096]{1,0:T(8,128)(2,1)S(1)} fusion(bf16[256,1536]{0,1:T(8,128)(2,1)} %bitcast.195, bf16[4096,2048]{0,1:T(8,128)(2,1)} %all-gather.2.cloned.1.call-done), kind=kOutput, calls=%fused_computation.9 | convolution fusion | flops 3222274048 | bytes 15466496 | tf_op jit(solution)/shard_map/dot_general | solution.py:182
  290.5 30.1 %all_to_all.52 = bf16[8,256,512]{2,1,0:T(8,128)(2,1)S(1)} all-to-all(bf16[8,256,512]{2,1,0:T(8,128)(2,1)S(1)} %bitcast.182), channel_id=1, replica_groups=mesh['section'=2,'dp'=8,'ctx'=8] {'dp'}, dimensions={0} | all-to-all | bytes 4194304 | tf_op jit(solution)/shard_map/all_to_all | solution.py:49
  321.7 8.9 %all_to_all.53 = f32[8,1,256]{2,1,0:T(1,128)S(1)} all-to-all(f32[8,1,256]{2,1,0:T(1,128)S(1)} %broadcast_in_dim.75), channel_id=1, replica_groups=mesh['section'=2,'dp'=8,'ctx'=8] {'dp'}, dimensions={0} | all-to-all | bytes 16384 | tf_op jit(solution)/shard_map/all_to_all | solution.py:28
  333.2 8.4 %collective-permute-done.7 = bf16[256,512]{1,0:T(8,128)(2,1)S(1)} collective-permute-done((bf16[256,512]{1,0:T(8,128)(2,1)S(1)}, bf16[256,512]{1,0:T(8,128)(2,1)S(1)}, u32[]{:S(2)}, u32[]{:S(2)}) %collective-permute-start.7) | collective-permute-done | bytes 262176 | tf_op jit(solution)/shard_map/ppermute | solution.py:38
  341.9 30.2 %all_to_all.54 = bf16[8,256,512]{1,2,0:T(8,128)(2,1)S(1)} all-to-all(bf16[8,256,512]{1,2,0:T(8,128)(2,1)S(1)} %broadcast_in_dim.76), channel_id=1, replica_groups=mesh['section'=2,'dp'=8,'ctx'=8] {'dp'}, dimensions={0} | all-to-all | bytes 4194304 | tf_op jit(solution)/shard_map/all_to_all | solution.py:28
  372.1 4.4 fusion.43
  378.0 3.9 collective-permute-start.8
  386.6 5.3 fusion.30
  404.0 8.0 %convolution_convert_fusion = bf16[4096,3,512]{2,0,1:T(8,128)(2,1)} fusion(bf16[256,4096,1]{0,1,2:T(8,128)(2,1)} %bitcast.183, bf16[256,3,512]{0,2,1:T(8,128)(2,1)S(1)} %copy.184), kind=kOutput, calls=%fused_computation.6 | convolution fusion | flops 3227516928 | bytes 15466496 | tf_op jit(solution)/shard_map/dot_general | solution.py:222
  415.0 5.3 fusion.44
  425.6 5.3 fusion.46
  441.7 5.6 %all-to-all-done.9 = bf16[8,3,3,512]{3,2,1,0:T(4,128)(2,1)S(1)} async-done(((bf16[8,3,3,512]{3,2,1,0:T(4,128)(2,1)}), bf16[8,3,3,512]{3,2,1,0:T(4,128)(2,1)S(1)}, u32[]{:S(2)}, u32[]{:S(2)}) %all-to-all-start.9) | async-done | bytes 73760 | tf_op jit(solution)/shard_map/all_to_all | solution.py:28
  448.3 4.4 all-to-all-start.8
  460.2 13.5 %all-to-all-done.8 = bf16[8,128,512]{2,1,0:T(8,128)(2,1)S(1)} async-done(((bf16[8,128,512]{2,1,0:T(8,128)(2,1)}), bf16[8,128,512]{2,1,0:T(8,128)(2,1)S(1)}, u32[]{:S(2)}, u32[]{:S(2)}) %all-to-all-start.8) | async-done | bytes 1048608 | tf_op jit(solution)/shard_map/all_to_all | solution.py:28
  473.8 5.5 all-to-all-start.7
  481.8 54.3 %all-to-all-done.7 = bf16[8,512,512]{2,1,0:T(8,128)(2,1)} async-done(((bf16[8,512,512]{2,1,0:T(8,128)(2,1)}), bf16[8,512,512]{2,1,0:T(8,128)(2,1)}, u32[]{:S(2)}, u32[]{:S(2)}) %all-to-all-start.7) | async-done | bytes 4194336 | tf_op jit(solution)/shard_map/all_to_all | solution.py:49
  (214 shorter events, 130.7 us)
Async XLA Ops:
  7.2 92.0 %all-gather.2.cloned.1.call-start = ((), (), s32[]{:S(2)}) async-start(), calls=%async_computation.11 | async-start | bytes 18874368 | tf_op jit(solution)/shard_map/all_gather | solution.py:12
  13.2 8.5 %copy-start.44 = (f32[1,512]{1,0:T(1,128)S(1)}, f32[1,512]{1,0:T(1,128)}, u32[]{:S(2)}) copy-start(f32[1,512]{1,0:T(1,128)} %param.13) | copy-start | bytes 6148
  13.2 8.5 %copy-start.41 = (f32[1,3,3,512]{3,0,2,1:T(1,128)S(1)}, f32[1,3,3,512]{3,0,2,1:T(1,128)}, u32[]{:S(2)}) copy-start(f32[1,3,3,512]{3,0,2,1:T(1,128)} %param.11) | copy-start | bytes 55300
  13.2 8.5 %copy-start.20 = (f32[1,128,512]{2,1,0:T(8,128)S(1)}, f32[1,128,512]{2,1,0:T(8,128)}, u32[]{:S(2)}) copy-start(f32[1,128,512]{2,1,0:T(8,128)} %param.12) | copy-start | bytes 786436
  13.2 37.1 %all-to-all-start = ((bf16[8,256,512]{1,2,0:T(8,128)(2,1)}), bf16[8,256,512]{1,2,0:T(8,128)(2,1)S(1)}, u32[]{:S(2)}, u32[]{:S(2)}) async-start(bf16[8,256,512]{1,2,0:T(8,128)(2,1)} %broadcast_in_dim.68), calls=%async_computation | async-start | bytes 4194304 | tf_op jit(solution)/shard_map/all_to_all | solution.py:28
  21.7 232.5 %copy-start.39 = (f32[1,512]{1,0:T(1,128)}, f32[1,512]{1,0:T(1,128)S(1)}, u32[]{:S(2)}) copy-start(f32[1,512]{1,0:T(1,128)S(1)} %neg.14) | copy-start | bytes 6148
  21.7 232.5 %copy-start.42 = (f32[128]{0:T(128)}, f32[128]{0:T(128)S(1)}, u32[]{:S(2)}) copy-start(f32[128]{0:T(128)S(1)} %iota_convert_fusion) | copy-start | bytes 1540
  107.5 9.1 %collective-permute-start = (f32[2,3,512]{2,0,1:T(2,128)S(1)}, f32[2,3,512]{2,0,1:T(2,128)S(1)}, u32[]{:S(2)}, u32[]{:S(2)}) collective-permute-start(f32[2,3,512]{2,0,1:T(2,128)S(1)} %bitcast.214), channel_id=1, source_target_pairs={{0,1},{1,2},{2,3},{3,4},{4,5},{5,6},{6,7},{8,9},{9,10},{10,11},{11... | collective-permute-start | bytes 36872 | tf_op jit(solution)/shard_map/ppermute | solution.py:38
  119.9 11.1 %copy-start.2 = (f32[256,3,512]{2,0,1:T(8,128)}, f32[256,3,512]{2,0,1:T(8,128)S(1)}, u32[]{:S(2)}) copy-start(f32[256,3,512]{2,0,1:T(8,128)S(1)} %multiply_add_fusion.1) | copy-start | bytes 4718596
  120.1 4.1 collective-permute-start.1
  170.6 7.5 %collective-permute-start.2 = (bf16[256,512]{1,0:T(8,128)(2,1)S(1)}, bf16[256,512]{1,0:T(8,128)(2,1)S(1)}, u32[]{:S(2)}, u32[]{:S(2)}) collective-permute-start(bf16[256,512]{1,0:T(8,128)(2,1)S(1)} %add_convert_fusion), channel_id=1, source_target_pairs={{0,64},{1,65},{2,66},{3,67},{4,68},{5,69},{6,70},{7,71},{8,72},{9,... | collective-permute-start | bytes 786440 | tf_op jit(solution)/shard_map/ppermute | solution.py:38
  179.7 33.1 %all-to-all-start.2 = ((bf16[8,256,512]{1,2,0:T(8,128)(2,1)}), bf16[8,256,512]{1,2,0:T(8,128)(2,1)}, u32[]{:S(2)}, u32[]{:S(2)}) async-start(bf16[8,256,512]{1,2,0:T(8,128)(2,1)} %broadcast_in_dim.71), calls=%async_computation.2 | async-start | bytes 4194304 | tf_op jit(solution)/shard_map/all_to_all | solution.py:28
  214.3 33.0 %all-to-all-start.3 = ((bf16[8,256,512]{1,2,0:T(8,128)(2,1)}), bf16[8,256,512]{1,2,0:T(8,128)(2,1)}, u32[]{:S(2)}, u32[]{:S(2)}) async-start(bf16[8,256,512]{1,2,0:T(8,128)(2,1)} %broadcast_in_dim.72), calls=%async_computation.3 | async-start | bytes 4194304 | tf_op jit(solution)/shard_map/all_to_all | solution.py:28
  218.7 321.3 %reduce-scatter.2.cloned.1.call-start = ((), (), s32[]{:S(2)}) async-start(), calls=%async_computation.12 | async-start | bytes 14155776 | tf_op jit(solution)/shard_map/reduce_scatter | solution.py:221
  231.1 8.0 %collective-permute-start.3 = (f32[2,3,512]{2,0,1:T(2,128)S(1)}, f32[2,3,512]{2,0,1:T(2,128)S(1)}, u32[]{:S(2)}, u32[]{:S(2)}) collective-permute-start(f32[2,3,512]{2,0,1:T(2,128)S(1)} %bitcast.215), channel_id=1, source_target_pairs={{0,1},{1,2},{2,3},{3,4},{4,5},{5,6},{6,7},{8,9},{9,10},{10,11},{11... | collective-permute-start | bytes 36872 | tf_op jit(solution)/shard_map/ppermute | solution.py:38
  251.5 11.8 %copy-start.28 = (f32[256,512]{1,0:T(8,128)}, f32[256,512]{1,0:T(8,128)S(1)}, u32[]{:S(2)}) copy-start(f32[256,512]{1,0:T(8,128)S(1)} %get-tuple-element.38) | copy-start | bytes 1572868
  251.5 6.3 %collective-permute-start.5 = (bf16[127,512]{1,0:T(8,128)(2,1)S(1)}, bf16[127,512]{1,0:T(8,128)(2,1)S(1)}, u32[]{:S(2)}, u32[]{:S(2)}) collective-permute-start(bf16[127,512]{1,0:T(8,128)(2,1)S(1)} %slice.267), channel_id=1, source_target_pairs={{1,0},{2,1},{3,2},{4,3},{5,4},{6,5},{7,6},{9,8},{10,9},{11,10},{12... | collective-permute-start | bytes 390152 | tf_op jit(solution)/shard_map/ppermute | solution.py:38
  257.9 5.3 copy-start.8
  263.4 3.9 collective-permute-start.4
  273.7 6.2 %copy-start.6 = (f32[256,3,512]{2,0,1:T(8,128)S(1)}, f32[256,3,512]{2,0,1:T(8,128)}, u32[]{:S(2)}) copy-start(f32[256,3,512]{2,0,1:T(8,128)} %copy.172) | copy-start | bytes 4718596
  273.7 6.0 %collective-permute-start.6 = (f32[2,3,512]{2,0,1:T(2,128)S(1)}, f32[2,3,512]{2,0,1:T(2,128)S(1)}, u32[]{:S(2)}, u32[]{:S(2)}) collective-permute-start(f32[2,3,512]{2,0,1:T(2,128)S(1)} %slice.161), channel_id=1, source_target_pairs={{1,0},{2,1},{3,2},{4,3},{5,4},{6,5},{7,6},{9,8},{10,9},{11,10},{12... | collective-permute-start | bytes 36872 | tf_op jit(solution)/shard_map/ppermute | solution.py:38
  331.9 9.7 %collective-permute-start.7 = (bf16[256,512]{1,0:T(8,128)(2,1)S(1)}, bf16[256,512]{1,0:T(8,128)(2,1)S(1)}, u32[]{:S(2)}, u32[]{:S(2)}) collective-permute-start(bf16[256,512]{1,0:T(8,128)(2,1)S(1)} %fusion.37), channel_id=1, source_target_pairs={{64,0},{65,1},{66,2},{67,3},{68,4},{69,5},{70,6},{71,7},{72,8},{73... | collective-permute-start | bytes 786440 | tf_op jit(solution)/shard_map/ppermute | solution.py:38
  341.9 30.2 %copy-start.25 = (f32[1,256,512]{2,0,1:T(1,128)S(1)}, f32[1,256,512]{2,0,1:T(1,128)}, u32[]{:S(2)}) copy-start(f32[1,256,512]{2,0,1:T(1,128)} %copy-done.24) | copy-start | bytes 1572868
  378.0 6.6 %collective-permute-start.8 = (bf16[127,512]{1,0:T(8,128)(2,1)}, bf16[127,512]{1,0:T(8,128)(2,1)}, u32[]{:S(2)}, u32[]{:S(2)}) collective-permute-start(bf16[127,512]{1,0:T(8,128)(2,1)} %slice.266), channel_id=1, source_target_pairs={{1,0},{2,1},{3,2},{4,3},{5,4},{6,5},{7,6},{9,8},{10,9},{11,10},{12... | collective-permute-start | bytes 390152 | tf_op jit(solution)/shard_map/ppermute | solution.py:38
  395.1 5.8 %collective-permute-start.9 = (f32[2,3,512]{2,0,1:T(2,128)S(1)}, f32[2,3,512]{2,0,1:T(2,128)S(1)}, u32[]{:S(2)}, u32[]{:S(2)}) collective-permute-start(f32[2,3,512]{2,0,1:T(2,128)S(1)} %slice.165), channel_id=1, source_target_pairs={{1,0},{2,1},{3,2},{4,3},{5,4},{6,5},{7,6},{9,8},{10,9},{11,10},{12... | collective-permute-start | bytes 36872 | tf_op jit(solution)/shard_map/ppermute | solution.py:38
  425.6 5.5 copy-start.17
  438.2 9.1 %all-to-all-start.9 = ((bf16[8,3,3,512]{3,2,1,0:T(4,128)(2,1)}), bf16[8,3,3,512]{3,2,1,0:T(4,128)(2,1)S(1)}, u32[]{:S(2)}, u32[]{:S(2)}) async-start(bf16[8,3,3,512]{3,2,1,0:T(4,128)(2,1)} %broadcast_in_dim.84), calls=%async_computation.10 | async-start | bytes 196608 | tf_op jit(solution)/shard_map/all_to_all | solution.py:28
  448.3 25.4 %all-to-all-start.8 = ((bf16[8,128,512]{2,1,0:T(8,128)(2,1)}), bf16[8,128,512]{2,1,0:T(8,128)(2,1)S(1)}, u32[]{:S(2)}, u32[]{:S(2)}) async-start(bf16[8,128,512]{2,1,0:T(8,128)(2,1)} %broadcast_in_dim.83), calls=%async_computation.9 | async-start | bytes 2097152 | tf_op jit(solution)/shard_map/all_to_all | solution.py:28
  473.8 6.3 %copy-start.40 = (f32[1,512]{1,0:T(1,128)S(1)}, f32[1,512]{1,0:T(1,128)}, u32[]{:S(2)}) copy-start(f32[1,512]{1,0:T(1,128)} %copy-done.39) | copy-start | bytes 6148
  473.8 6.3 %copy-start.43 = (f32[128]{0:T(128)S(1)}, f32[128]{0:T(128)}, u32[]{:S(2)}) copy-start(f32[128]{0:T(128)} %copy-done.42) | copy-start | bytes 1540
  473.8 62.3 %all-to-all-start.7 = ((bf16[8,512,512]{2,1,0:T(8,128)(2,1)}), bf16[8,512,512]{2,1,0:T(8,128)(2,1)}, u32[]{:S(2)}, u32[]{:S(2)}) async-start(bf16[8,512,512]{2,1,0:T(8,128)(2,1)} %bitcast.178), calls=%async_computation.8 | async-start | bytes 8388608 | tf_op jit(solution)/shard_map/all_to_all | solution.py:49
  536.1 7.4 %copy-start.1 = (bf16[512,512]{1,0:T(8,128)(2,1)S(1)}, bf16[512,512]{1,0:T(8,128)(2,1)}, u32[]{:S(2)}) copy-start(bf16[512,512]{1,0:T(8,128)(2,1)} %param.9) | copy-start | bytes 1572868
  (32 other events, 78.5 us)
Sparse Core Ops, SparseCore 0:
  10.7 88.4 all-gather.1
  412.1 95.6 reduce-scatter.1
where the time goes:
time: 560 us; the launch traced here: 551 us
  waiting for transfers between devices  208 us (37%)
  blocking collectives  105 us (19%)
  matrix products  75.8 us (14%)
  starting transfers between devices  54.7 us (10%)
  local copies, waits for them, and re-layouts  49.2 us (9%)
  other arithmetic  43.2 us (8%)
  between operations  15.2 us (3%)
    all_to_all x5, waiting for transfers between devices, from_everyone(): return lax.all_to_all(copies, axis, split_axis=0, concat_axis=0, tiled=True)  79.9 us
    all_to_all x2, blocking collectives, summed_on_arrival(): lax.all_to_all(cut_along(shard, dim, peers), axis, 0, 0, tiled=True)  65.4 us
    all_to_all x1, waiting for transfers between devices, summed_on_arrival(): lax.all_to_all(cut_along(shard, dim, peers), axis, 0, 0, tiled=True)  54.3 us
    all_gather x1, waiting for transfers between devices, gather_turned(): lax.all_gather(both, axis, axis=0, tiled=True)  46.5 us
    all_to_all x2, blocking collectives, from_everyone(): return lax.all_to_all(copies, axis, split_axis=0, concat_axis=0, tiled=True)  39.1 us
    conv_general_dilated x6, matrix products, correlate(): lax.conv_general_dilated(signal[None], kernel[:, None, :], (1,), 'VALID',...  31.8 us
    ppermute x10, waiting for transfers between devices, from_behind(): lax.ppermute(value, axis, [(source, source + steps) for source in range(i...  27 us
    all_to_all x5, starting transfers between devices, from_everyone(): return lax.all_to_all(copies, axis, split_axis=0, concat_axis=0, tiled=True)  25.1 us
  transfers between devices with their start and end apart: 18, of which 14 were waited for; matrix products, arithmetic and copies ran while one was open for 13% of the time, Pallas kernels for 0%

commit v1 on v0

--- a/solution.py
+++ b/solution.py
@@ -9,7 +9,11 @@
 def gather_turned(arrays, axis, dims):
     turned = [jnp.moveaxis(a, dim, 0) for a, dim in zip(arrays, dims)]
     both = jnp.concatenate([t.reshape(len(t), -1) for t in turned], axis=1)
-    filled, at, finished = (lax.all_gather(both, axis, axis=0, tiled=True), 0, [])
+    _clear_rows = lambda obj, which_axis: jnp.concatenate(
+        lax.all_to_all(jnp.stack([obj] * lax.axis_size(which_axis), axis=0), which_axis, 0, 0),
+        axis=0,
+    )
+    filled, at, finished = (_clear_rows(both, axis), 0, [])
     for t, dim in zip(turned, dims):
         section = filled[:, at : at + t[0].size].reshape(-1, *t.shape[1:])
         finished.append(jnp.moveaxis(section, 0, dim))

time: 560 us -> 708 us (1.26)
  waiting for transfers between devices: 208 us -> 333 us
  local copies, waits for them, and re-layouts: 49.2 us -> 61.4 us
  starting transfers between devices: 54.7 us -> 61.9 us
    all_to_all x0 -> x1, waiting for transfers between devices: none -> 181 us  [gather_turned(): lax.all_to_all(jnp.stack([obj] * lax.axis_size(which_axis), axis=0), whic...]
    all_gather x1 -> x0, waiting for transfers between devices: 46.5 us -> none  [gather_turned(): lax.all_gather(both, axis, axis=0, tiled=True)]
    all_to_all x5, waiting for transfers between devices: 79.9 us -> 70.8 us  [from_everyone(): return lax.all_to_all(copies, axis, split_axis=0, concat_axis=0, tiled=True)]
    unnamed x99 -> x97, local copies, waits for them, and re-layouts: 13.8 us -> 15 us
  transfers between devices with their start and end apart: 18 -> 18, of which waited for: 14 -> 14; matrix products, arithmetic and copies ran while one was open for 13% -> 12% of each run, Pallas kernels for 0% -> 0%
where the time goes in v1:
time: 708 us; the launch traced here: 698 us
  waiting for transfers between devices  333 us (47%)
  blocking collectives  106 us (15%)
  matrix products  76.4 us (11%)
  starting transfers between devices  61.9 us (9%)
  local copies, waits for them, and re-layouts  61.4 us (9%)
  other arithmetic  44.4 us (6%)
  between operations  15.2 us (2%)
    all_to_all x1, waiting for transfers between devices, gather_turned(): lax.all_to_all(jnp.stack([obj] * lax.axis_size(which_axis), axis=0), whic...  181 us
    all_to_all x5, waiting for transfers between devices, from_everyone(): return lax.all_to_all(copies, axis, split_axis=0, concat_axis=0, tiled=True)  70.8 us
    all_to_all x2, blocking collectives, summed_on_arrival(): lax.all_to_all(cut_along(shard, dim, peers), axis, 0, 0, tiled=True)  66.4 us
    all_to_all x1, waiting for transfers between devices, summed_on_arrival(): lax.all_to_all(cut_along(shard, dim, peers), axis, 0, 0, tiled=True)  54.3 us
    all_to_all x2, blocking collectives, from_everyone(): return lax.all_to_all(copies, axis, split_axis=0, concat_axis=0, tiled=True)  39.1 us
    conv_general_dilated x6, matrix products, correlate(): lax.conv_general_dilated(signal[None], kernel[:, None, :], (1,), 'VALID',...  31.8 us
    ppermute x10, waiting for transfers between devices, from_behind(): lax.ppermute(value, axis, [(source, source + steps) for source in range(i...  26.8 us
    all_to_all x5, starting transfers between devices, from_everyone(): return lax.all_to_all(copies, axis, split_axis=0, concat_axis=0, tiled=True)  25.5 us
  transfers between devices with their start and end apart: 18, of which 14 were waited for; matrix products, arithmetic and copies ran while one was open for 12% of the time, Pallas kernels for 0%

profile of v1, /device:TPU:1, one launch (start us, length us, event | category | flops | bytes accessed | tf_op | source)
XLA Modules:
  0.0 697.9 jit_solution(632705426574937655)
XLA Ops:
  10.9 8.3 %all-to-all-start = ((bf16[8,256,512]{1,2,0:T(8,128)(2,1)}), bf16[8,256,512]{1,2,0:T(8,128)(2,1)S(1)}, u32[]{:S(2)}, u32[]{:S(2)}) async-start(bf16[8,256,512]{1,2,0:T(8,128)(2,1)} %broadcast_in_dim.68), calls=%async_computation | async-start | bytes 4194304 | tf_op jit(solution)/shard_map/all_to_all | solution.py:32
  28.7 19.1 %all-to-all-done = bf16[8,256,512]{1,2,0:T(8,128)(2,1)S(1)} async-done(((bf16[8,256,512]{1,2,0:T(8,128)(2,1)}), bf16[8,256,512]{1,2,0:T(8,128)(2,1)S(1)}, u32[]{:S(2)}, u32[]{:S(2)}) %all-to-all-start) | async-done | bytes 2097184 | tf_op jit(solution)/shard_map/all_to_all | solution.py:32
  47.8 7.0 stack.55
  54.8 6.6 all-to-all-start.1
  63.9 181.1 %all-to-all-done.1 = bf16[8,512,2048]{2,1,0:T(8,128)(2,1)} async-done(((bf16[8,512,2048]{2,1,0:T(8,128)(2,1)}), bf16[8,512,2048]{2,1,0:T(8,128)(2,1)}, u32[]{:S(2)}, u32[]{:S(2)}) %all-to-all-start.1) | async-done | bytes 16777248 | tf_op jit(solution)/shard_map/all_to_all | solution.py:13
  245.0 7.1 %fusion.4 = f32[256,1536]{1,0:T(8,128)S(1)} fusion(bf16[256,4096]{0,1:T(8,128)(2,1)} %fusion.10, bf16[4096,2048]{1,0:T(8,128)(2,1)} %bitcast.5), kind=kOutput, calls=%fused_computation.4 | convolution fusion | flops 3221225472 | bytes 16252928 | tf_op jit(solution)/shard_map/dot_general | solution.py:108
  271.4 5.3 fusion.64
  280.6 34.3 %all_to_all.56 = bf16[8,256,512]{2,1,0:T(8,128)(2,1)S(1)} all-to-all(bf16[8,256,512]{2,1,0:T(8,128)(2,1)S(1)} %bitcast.182), channel_id=1, replica_groups=mesh['section'=2,'dp'=8,'ctx'=8] {'dp'}, dimensions={0} | all-to-all | bytes 4194304 | tf_op jit(solution)/shard_map/all_to_all | solution.py:53
  318.0 5.0 collective-permute-done.2
  324.5 4.5 all-to-all-start.3
  329.2 28.5 %all-to-all-done.3 = bf16[8,256,512]{1,2,0:T(8,128)(2,1)} async-done(((bf16[8,256,512]{1,2,0:T(8,128)(2,1)}), bf16[8,256,512]{1,2,0:T(8,128)(2,1)}, u32[]{:S(2)}, u32[]{:S(2)}) %all-to-all-start.3) | async-done | bytes 2097184 | tf_op jit(solution)/shard_map/all_to_all | solution.py:32
  359.1 4.4 all-to-all-start.4
  368.2 6.5 fusion.2
  383.9 4.3 multiply_add_fusion
  392.1 4.2 bitcast_multiply_fusion.11
  402.8 5.3 fusion.32
  412.3 5.3 fusion.49
  426.9 8.3 %fusion.6 = bf16[256,4096]{1,0:T(8,128)(2,1)S(1)} fusion(bf16[256,1536]{0,1:T(8,128)(2,1)} %bitcast.196, bf16[4096,2048]{1,0:T(8,128)(2,1)} %bitcast.5), kind=kOutput, calls=%fused_computation.9 | convolution fusion | flops 3222274048 | bytes 15466496 | tf_op jit(solution)/shard_map/dot_general | solution.py:186
  435.4 32.2 %all_to_all.57 = bf16[8,256,512]{2,1,0:T(8,128)(2,1)S(1)} all-to-all(bf16[8,256,512]{2,1,0:T(8,128)(2,1)S(1)} %bitcast.183), channel_id=1, replica_groups=mesh['section'=2,'dp'=8,'ctx'=8] {'dp'}, dimensions={0} | all-to-all | bytes 4194304 | tf_op jit(solution)/shard_map/all_to_all | solution.py:53
  468.7 8.9 %all_to_all.58 = f32[8,1,256]{2,1,0:T(1,128)S(1)} all-to-all(f32[8,1,256]{2,1,0:T(1,128)S(1)} %broadcast_in_dim.75), channel_id=1, replica_groups=mesh['section'=2,'dp'=8,'ctx'=8] {'dp'}, dimensions={0} | all-to-all | bytes 16384 | tf_op jit(solution)/shard_map/all_to_all | solution.py:32
  480.2 8.4 %collective-permute-done.7 = bf16[256,512]{1,0:T(8,128)(2,1)S(1)} collective-permute-done((bf16[256,512]{1,0:T(8,128)(2,1)S(1)}, bf16[256,512]{1,0:T(8,128)(2,1)S(1)}, u32[]{:S(2)}, u32[]{:S(2)}) %collective-permute-start.7) | collective-permute-done | bytes 262176 | tf_op jit(solution)/shard_map/ppermute | solution.py:42
  488.8 30.2 %all_to_all.59 = bf16[8,256,512]{1,2,0:T(8,128)(2,1)S(1)} all-to-all(bf16[8,256,512]{1,2,0:T(8,128)(2,1)S(1)} %broadcast_in_dim.76), channel_id=1, replica_groups=mesh['section'=2,'dp'=8,'ctx'=8] {'dp'}, dimensions={0} | all-to-all | bytes 4194304 | tf_op jit(solution)/shard_map/all_to_all | solution.py:32
  519.1 4.3 fusion.43
  533.5 5.3 fusion.30
  550.9 8.0 %convolution_convert_fusion = bf16[4096,3,512]{2,0,1:T(8,128)(2,1)} fusion(bf16[256,4096,1]{0,1,2:T(8,128)(2,1)} %bitcast.184, bf16[256,3,512]{0,2,1:T(8,128)(2,1)S(1)} %copy.189), kind=kOutput, calls=%fused_computation.6 | convolution fusion | flops 3227516928 | bytes 15466496 | tf_op jit(solution)/shard_map/dot_general | solution.py:226
  562.0 5.3 fusion.44
  572.5 5.3 fusion.46
  589.0 5.6 all-to-all-done.10
  595.7 4.4 all-to-all-start.9
  607.6 13.6 %all-to-all-done.9 = bf16[8,128,512]{2,1,0:T(8,128)(2,1)S(1)} async-done(((bf16[8,128,512]{2,1,0:T(8,128)(2,1)}), bf16[8,128,512]{2,1,0:T(8,128)(2,1)S(1)}, u32[]{:S(2)}, u32[]{:S(2)}) %all-to-all-start.9) | async-done | bytes 1048608 | tf_op jit(solution)/shard_map/all_to_all | solution.py:32
  621.1 5.5 all-to-all-start.8
  629.2 54.3 %all-to-all-done.8 = bf16[8,512,512]{2,1,0:T(8,128)(2,1)} async-done(((bf16[8,512,512]{2,1,0:T(8,128)(2,1)}), bf16[8,512,512]{2,1,0:T(8,128)(2,1)}, u32[]{:S(2)}, u32[]{:S(2)}) %all-to-all-start.8) | async-done | bytes 4194336 | tf_op jit(solution)/shard_map/all_to_all | solution.py:53
  (213 shorter events, 146.5 us)
Async XLA Ops:
  10.9 36.9 %all-to-all-start = ((bf16[8,256,512]{1,2,0:T(8,128)(2,1)}), bf16[8,256,512]{1,2,0:T(8,128)(2,1)S(1)}, u32[]{:S(2)}, u32[]{:S(2)}) async-start(bf16[8,256,512]{1,2,0:T(8,128)(2,1)} %broadcast_in_dim.68), calls=%async_computation | async-start | bytes 4194304 | tf_op jit(solution)/shard_map/all_to_all | solution.py:32
  54.8 6.6 copy-start.44
  54.8 6.6 copy-start.41
  54.8 6.6 copy-start.20
  54.8 190.2 %all-to-all-start.1 = ((bf16[8,512,2048]{2,1,0:T(8,128)(2,1)}), bf16[8,512,2048]{2,1,0:T(8,128)(2,1)}, u32[]{:S(2)}, u32[]{:S(2)}) async-start(bf16[8,512,2048]{2,1,0:T(8,128)(2,1)} %stack.55), calls=%async_computation.1 | async-start | bytes 33554432 | tf_op jit(solution)/shard_map/all_to_all | solution.py:13
  61.3 337.7 %copy-start.39 = (f32[1,512]{1,0:T(1,128)}, f32[1,512]{1,0:T(1,128)S(1)}, u32[]{:S(2)}) copy-start(f32[1,512]{1,0:T(1,128)S(1)} %neg.14) | copy-start | bytes 6148
  61.4 337.7 %copy-start.42 = (f32[128]{0:T(128)}, f32[128]{0:T(128)S(1)}, u32[]{:S(2)}) copy-start(f32[128]{0:T(128)S(1)} %iota_convert_fusion) | copy-start | bytes 1540
  253.3 9.3 %collective-permute-start = (f32[2,3,512]{2,0,1:T(2,128)S(1)}, f32[2,3,512]{2,0,1:T(2,128)S(1)}, u32[]{:S(2)}, u32[]{:S(2)}) collective-permute-start(f32[2,3,512]{2,0,1:T(2,128)S(1)} %bitcast.215), channel_id=1, source_target_pairs={{0,1},{1,2},{2,3},{3,4},{4,5},{5,6},{6,7},{8,9},{9,10},{10,11},{11... | collective-permute-start | bytes 36872 | tf_op jit(solution)/shard_map/ppermute | solution.py:42
  265.9 10.8 %copy-start.2 = (f32[256,3,512]{2,0,1:T(8,128)}, f32[256,3,512]{2,0,1:T(8,128)S(1)}, u32[]{:S(2)}) copy-start(f32[256,3,512]{2,0,1:T(8,128)S(1)} %multiply_add_fusion.1) | copy-start | bytes 4718596
  266.0 3.9 collective-permute-start.1
  315.3 7.6 %collective-permute-start.2 = (bf16[256,512]{1,0:T(8,128)(2,1)S(1)}, bf16[256,512]{1,0:T(8,128)(2,1)S(1)}, u32[]{:S(2)}, u32[]{:S(2)}) collective-permute-start(bf16[256,512]{1,0:T(8,128)(2,1)S(1)} %add_convert_fusion), channel_id=1, source_target_pairs={{0,64},{1,65},{2,66},{3,67},{4,68},{5,69},{6,70},{7,71},{8,72},{9,... | collective-permute-start | bytes 786440 | tf_op jit(solution)/shard_map/ppermute | solution.py:42
  324.5 33.1 %all-to-all-start.3 = ((bf16[8,256,512]{1,2,0:T(8,128)(2,1)}), bf16[8,256,512]{1,2,0:T(8,128)(2,1)}, u32[]{:S(2)}, u32[]{:S(2)}) async-start(bf16[8,256,512]{1,2,0:T(8,128)(2,1)} %broadcast_in_dim.71), calls=%async_computation.3 | async-start | bytes 4194304 | tf_op jit(solution)/shard_map/all_to_all | solution.py:32
  359.1 33.0 %all-to-all-start.4 = ((bf16[8,256,512]{1,2,0:T(8,128)(2,1)}), bf16[8,256,512]{1,2,0:T(8,128)(2,1)}, u32[]{:S(2)}, u32[]{:S(2)}) async-start(bf16[8,256,512]{1,2,0:T(8,128)(2,1)} %broadcast_in_dim.72), calls=%async_computation.4 | async-start | bytes 4194304 | tf_op jit(solution)/shard_map/all_to_all | solution.py:32
  363.5 323.8 %reduce-scatter.2.cloned.1.call-start = ((), (), s32[]{:S(2)}) async-start(), calls=%async_computation.12 | async-start | bytes 14155776 | tf_op jit(solution)/shard_map/reduce_scatter | solution.py:225
  375.9 8.0 %collective-permute-start.3 = (f32[2,3,512]{2,0,1:T(2,128)S(1)}, f32[2,3,512]{2,0,1:T(2,128)S(1)}, u32[]{:S(2)}, u32[]{:S(2)}) collective-permute-start(f32[2,3,512]{2,0,1:T(2,128)S(1)} %bitcast.216), channel_id=1, source_target_pairs={{0,1},{1,2},{2,3},{3,4},{4,5},{5,6},{6,7},{8,9},{9,10},{10,11},{11... | collective-permute-start | bytes 36872 | tf_op jit(solution)/shard_map/ppermute | solution.py:42
  396.3 11.8 %copy-start.28 = (f32[256,512]{1,0:T(8,128)}, f32[256,512]{1,0:T(8,128)S(1)}, u32[]{:S(2)}) copy-start(f32[256,512]{1,0:T(8,128)S(1)} %get-tuple-element.38) | copy-start | bytes 1572868
  396.4 6.3 collective-permute-start.5
  402.7 5.3 copy-start.8
  408.3 3.9 collective-permute-start.4
  418.6 6.2 copy-start.6
  418.6 6.0 collective-permute-start.6
  478.9 9.7 %collective-permute-start.7 = (bf16[256,512]{1,0:T(8,128)(2,1)S(1)}, bf16[256,512]{1,0:T(8,128)(2,1)S(1)}, u32[]{:S(2)}, u32[]{:S(2)}) collective-permute-start(bf16[256,512]{1,0:T(8,128)(2,1)S(1)} %fusion.37), channel_id=1, source_target_pairs={{64,0},{65,1},{66,2},{67,3},{68,4},{69,5},{70,6},{71,7},{72,8},{73... | collective-permute-start | bytes 786440 | tf_op jit(solution)/shard_map/ppermute | solution.py:42
  488.8 30.2 %copy-start.25 = (f32[1,256,512]{2,0,1:T(1,128)S(1)}, f32[1,256,512]{2,0,1:T(1,128)}, u32[]{:S(2)}) copy-start(f32[1,256,512]{2,0,1:T(1,128)} %copy-done.24) | copy-start | bytes 1572868
  524.9 6.6 collective-permute-start.8
  542.1 5.8 collective-permute-start.9
  572.5 5.5 copy-start.17
  585.1 9.5 %all-to-all-start.10 = ((bf16[8,3,3,512]{3,2,1,0:T(4,128)(2,1)}), bf16[8,3,3,512]{3,2,1,0:T(4,128)(2,1)S(1)}, u32[]{:S(2)}, u32[]{:S(2)}) async-start(bf16[8,3,3,512]{3,2,1,0:T(4,128)(2,1)} %broadcast_in_dim.84), calls=%async_computation.11 | async-start | bytes 196608 | tf_op jit(solution)/shard_map/all_to_all | solution.py:32
  595.7 25.4 %all-to-all-start.9 = ((bf16[8,128,512]{2,1,0:T(8,128)(2,1)}), bf16[8,128,512]{2,1,0:T(8,128)(2,1)S(1)}, u32[]{:S(2)}, u32[]{:S(2)}) async-start(bf16[8,128,512]{2,1,0:T(8,128)(2,1)} %broadcast_in_dim.83), calls=%async_computation.10 | async-start | bytes 2097152 | tf_op jit(solution)/shard_map/all_to_all | solution.py:32
  621.1 6.4 copy-start.40
  621.1 6.4 copy-start.43
  621.1 62.3 %all-to-all-start.8 = ((bf16[8,512,512]{2,1,0:T(8,128)(2,1)}), bf16[8,512,512]{2,1,0:T(8,128)(2,1)}, u32[]{:S(2)}, u32[]{:S(2)}) async-start(bf16[8,512,512]{2,1,0:T(8,128)(2,1)} %bitcast.179), calls=%async_computation.9 | async-start | bytes 8388608 | tf_op jit(solution)/shard_map/all_to_all | solution.py:53
  683.4 7.4 %copy-start.1 = (bf16[512,512]{1,0:T(8,128)(2,1)S(1)}, bf16[512,512]{1,0:T(8,128)(2,1)}, u32[]{:S(2)}) copy-start(bf16[512,512]{1,0:T(8,128)(2,1)} %param.9) | copy-start | bytes 1572868
  (31 other events, 76.2 us)
Sparse Core Ops, SparseCore 0:
  559.1 95.8 reduce-scatter.1
